TPU v7x, 32 devices: a whole 2x2x4 slice. The times are simulated.
32 devices in a mesh: groups: 2 (over y), expert: 4 (over x, core), hidden: 4 (over z).
Axes of the slice: x: 2, y: 2, z: 4, core: 2. Of those that a mesh axis runs over, the one named last changes fastest.
Arguments:
- tokens: bfloat16 [1024, 3072], P(('groups', 'expert'), 'hidden'), parts along dimension 0, may hold values from -6 to 6
- routes: int32 [1024, 2], P(('groups', 'expert')), parts along dimension 0, may hold values from 0 to 7, all different within a row; in each aligned block of 128 rows (0 to 127, 128 to 255, ...) at most 48 rows name the same one
- router_weight: bfloat16 [3072, 8], replicated, may hold values from -0.109375 to 0.109375
- gate_weight: bfloat16 [8, 3072, 8192], P('expert', None, 'hidden'), may hold values from -0.109375 to 0.109375
- up_weight: bfloat16 [8, 3072, 8192], P('expert', None, 'hidden'), may hold values from -0.109375 to 0.109375
- down_weight: bfloat16 [8, 8192, 3072], P('expert', 'hidden'), may hold values from -0.09375 to 0.09375
Outputs:
- mixed: bfloat16 [1024, 3072], P(('groups', 'expert'), 'hidden'), parts along dimension 0
There are 2 independent parts, one for each index of `groups`. A program takes and returns all parts, laid end to end along the dimension named above; an argument that names none is the same for every part. Nothing has to cross between parts.
Inputs may be any that keep to these rules, and one draw needn't show every extreme that they name: `routes`: each token names two different experts. Among the 128 tokens of one index of expert (aligned blocks of rows) no expert is named more than 48 times, a bound that some block reaches.
All inputs are finite; a program needn't handle non-finite values.
Results may differ from a plain program's by a relative error of at most 0.0057.
Values may be sent and summed in bfloat16 or wider, within the bound.
No kernel may reach another device: no remote copies, remote signals or barrier semaphores. Data moves between devices by JAX's collectives and lax.ppermute only.
A program may use at most 128 MiB of HBM per device.

v0:
```python
import jax
import jax.numpy as jnp
from jax import lax
from jax.sharding import PartitionSpec as P

CAP = 48


def per_device(tokens, routes, router_weight, gate_weight, up_weight, down_weight):
    experts_here = gate_weight.shape[0]
    groups = lax.axis_size("expert")
    experts_all = experts_here * groups
    local_tokens = tokens.shape[0]
    capacity = CAP
    flat_ids = routes.reshape(-1)
    onehot = (flat_ids[:, None] == jnp.arange(experts_all, dtype=jnp.int32)[None, :]).astype(
        jnp.int32
    )
    position = jnp.sum((jnp.cumsum(onehot, axis=0) - onehot) * onehot, axis=1)
    slot_of = flat_ids * capacity + position
    owners = jnp.arange(flat_ids.shape[0], dtype=jnp.int32) // 2
    inverse = jnp.full((experts_all * capacity,), local_tokens, jnp.int32).at[slot_of].set(owners)
    gathered = lax.all_gather(tokens, "hidden", axis=1, tiled=True)
    logits = jnp.dot(gathered, router_weight, preferred_element_type=jnp.float32)
    padded = jnp.concatenate([gathered, jnp.zeros((1, gathered.shape[1]), jnp.bfloat16)], axis=0)
    send_rows = padded[inverse].reshape(experts_all, 1, capacity, gathered.shape[1])
    arrived = lax.all_to_all(send_rows, "expert", split_axis=0, concat_axis=1, tiled=True)
    gate_act = jnp.einsum(
        "ensd,edf->ensf", arrived, gate_weight, preferred_element_type=jnp.float32
    )
    up_act = jnp.einsum("ensd,edf->ensf", arrived, up_weight, preferred_element_type=jnp.float32)
    hidden_act = (jax.nn.silu(gate_act) * up_act).astype(jnp.bfloat16)
    hidden_act = hidden_act.reshape(experts_here, groups * capacity, hidden_act.shape[3])
    partial_value = jnp.einsum(
        "erf,efd->erd", hidden_act, down_weight, preferred_element_type=jnp.float32
    )
    summed = lax.psum_scatter(partial_value, "hidden", scatter_dimension=2, tiled=True).astype(
        jnp.bfloat16
    )
    summed = summed.reshape(experts_here, groups, capacity, summed.shape[2])
    returned = lax.all_to_all(summed, "expert", split_axis=1, concat_axis=0, tiled=True)
    results = returned.reshape(experts_all * capacity, returned.shape[3])
    selected = jnp.take_along_axis(logits, routes, axis=1)
    share = jax.nn.sigmoid(selected[:, 0] - selected[:, 1])
    slot_pairs = slot_of.reshape(local_tokens, 2)
    first_out = results[slot_pairs[:, 0]].astype(jnp.float32)
    second_out = results[slot_pairs[:, 1]].astype(jnp.float32)
    mixture = share[:, None] * first_out + (1.0 - share)[:, None] * second_out
    return mixture.astype(jnp.bfloat16)


def solution(mesh):
    return jax.shard_map(
        per_device,
        mesh=mesh,
        in_specs=(
            P(("groups", "expert"), "hidden"),
            P(("groups", "expert"), None),
            P(),
            P("expert", None, "hidden"),
            P("expert", None, "hidden"),
            P("expert", "hidden", None),
        ),
        out_specs=P(("groups", "expert"), "hidden"),
        check_vma=False,
    )
```

profile of v0, /device:TPU:0, one launch (start us, length us, event | category | flops | bytes accessed | tf_op | source)
XLA Modules:
  0.0 209.8 jit_solution(10546477326377145028)
XLA Ops:
  6.5 0.0 copy-start
  6.5 0.0 reduce-scatter.2.cloned.1.call-start
  6.5 0.8 copy.41
  7.3 0.1 eq.29
  7.5 0.1 eq.25
  7.6 0.6 reduce-window.6
  8.2 0.2 slice_reduce_fusion
  8.5 0.1 fusion.13
  8.6 0.1 reduce_sum.15
  8.7 0.1 mul.51
  8.9 1.4 scatter_custom_fusion
  10.3 21.5 %all_gather.3 = bf16[128,3072]{1,0:T(8,128)(2,1)S(1)} all-gather(bf16[128,768]{1,0:T(8,128)(2,1)} %param.6), channel_id=1, replica_groups=mesh['groups'=2,'expert'=4,'hidden'=4] {'hidden'}, dimensions={1}, use_global_device_ids=true | all-gather | bytes 983040 | tf_op jit(solution)/shard_map/all_gather | solution.py:23
  31.8 0.0 copy-start.1
  31.8 0.9 copy-done.1
  32.7 0.1 concatenate.3
  32.8 2.9 %gather_fusion = bf16[384,3072]{1,0:T(8,128)(2,1)S(1)} fusion(bf16[129,3072]{1,0:T(8,128)(2,1)S(1)} %concatenate.3, s32[1024]{0:T(1024)S(1)} %pad_clamp_fusion.2), kind=kCustom, calls=%fused_computation | custom fusion | bytes 4720128 | tf_op jit(solution)/shard_map/gather | solution.py:26
  35.7 31.0 %all_to_all.33 = bf16[8,1,48,3072]{3,2,1,0:T(8,128)(2,1)S(1)} all-to-all(bf16[8,1,48,3072]{3,2,1,0:T(8,128)(2,1)S(1)} %bitcast.57), channel_id=1, replica_groups=mesh['groups'=2,'expert'=4,'hidden'=4] {'expert'}, dimensions={0} | all-to-all | bytes 4718592 | tf_op jit(solution)/shard_map/all_to_all | solution.py:27
  66.7 10.8 %fusion.2 = f32[2,4,48,2048]{3,2,1,0:T(8,128)S(1)} fusion(bf16[2,3072,2048]{2,1,0:T(8,128)(2,1)} %param.9, bf16[4,2,1,48,3072]{4,3,1,0,2:T(8,128)(2,1)S(1)} %bitcast.52), kind=kOutput, calls=%fused_computation.7 | convolution fusion | flops 4831838208 | bytes 30670848 | tf_op jit(solution)/shard_map/ensd,edf->ensf/dot_general | solution.py:28
  77.5 11.0 %multiply_convert_fusion = bf16[2,4,48,2048]{3,2,1,0:T(8,128)(2,1)S(1)} fusion(f32[2,4,48,2048]{3,2,1,0:T(8,128)S(1)} %fusion.2, bf16[2,3072,2048]{2,1,0:T(8,128)(2,1)} %param.10, bf16[4,2,1,48,3072]{4,3,1,0,2:T(8,128)(2,1)S(1)} %bitcast.53), kind=kOutput, calls=%fused_computation.9 | convolution fusion | flops 4836556800 | bytes 32243712 | tf_op jit(solution)/shard_map/ensd,edf->ensf/dot_general | solution.py:31
  88.5 12.9 %fusion.19 = f32[2,192,3072]{2,1,0:T(8,128)} fusion(bf16[2,192,2048]{2,1,0:T(8,128)(2,1)S(1)} %bitcast.56, bf16[2,2048,3072]{2,1,0:T(8,128)(2,1)} %param.11), kind=kOutput, calls=%fused_computation.45 | convolution fusion | flops 4831838208 | bytes 31457280 | tf_op jit(solution)/shard_map/erf,efd->erd/dot_general | solution.py:34
  101.4 0.0 copy-start.3
  101.4 0.0 copy-start.2
  101.4 0.0 reduce-scatter.2.cloned.1.call-update
  101.5 0.7 copy-done.3
  102.1 0.1 copy.39
  102.2 0.1 reshape.100
  102.4 0.0 copy-done
  102.4 0.2 copy-done.2
  102.6 0.3 fusion.18
  102.9 1.4 gather_fusion.3
  104.3 0.1 reshape.103
  104.4 0.1 copy.40
  104.5 0.2 fusion.10
  104.7 80.6 %reduce-scatter.2.cloned.1.call-done = f32[2,192,768]{2,1,0:T(8,128)} async-done(((f32[2,192,3072]{2,1,0:T(8,128)}), f32[2,192,768]{2,1,0:T(8,128)}) %reduce-scatter.2.cloned.1.call-update) | async-done | bytes 1179664 | tf_op jit(solution)/shard_map/reduce_scatter | solution.py:37
  185.3 1.3 convert_element_type.25
  186.6 0.8 copy.46
  187.5 3.5 %all-to-all-start.1 = ((bf16[2,4,48,768]{3,2,0,1:T(8,128)(2,1)}), bf16[2,4,48,768]{3,2,0,1:T(8,128)(2,1)S(1)}, u32[]{:S(2)}, u32[]{:S(2)}) async-start(bf16[2,4,48,768]{3,2,0,1:T(8,128)(2,1)} %copy.46), calls=%async_computation.2 | async-start | bytes 1179648 | tf_op jit(solution)/shard_map/all_to_all | solution.py:41
  191.0 9.5 %all-to-all-done.1 = bf16[2,4,48,768]{3,2,0,1:T(8,128)(2,1)S(1)} async-done(((bf16[2,4,48,768]{3,2,0,1:T(8,128)(2,1)}), bf16[2,4,48,768]{3,2,0,1:T(8,128)(2,1)S(1)}, u32[]{:S(2)}, u32[]{:S(2)}) %all-to-all-start.1) | async-done | bytes 589856 | tf_op jit(solution)/shard_map/all_to_all | solution.py:41
  200.4 0.9 gather_fusion.2
  201.3 0.9 gather_fusion.1
  202.2 0.8 add_convert_fusion
  (12 shorter events, 0.1 us)
Async XLA Ops:
  6.5 95.8 %copy-start = (bf16[3072,8]{0,1:T(8,128)(2,1)S(1)}, bf16[3072,8]{0,1:T(8,128)(2,1)}, u32[]{:S(2)}) copy-start(bf16[3072,8]{0,1:T(8,128)(2,1)} %param.8) | copy-start | bytes 147460
  6.5 178.8 %reduce-scatter.2.cloned.1.call-start = ((), (), s32[]{:S(2)}) async-start(), calls=%async_computation.3 | async-start | bytes 5898240 | tf_op jit(solution)/shard_map/reduce_scatter | solution.py:37
  31.8 0.9 copy-start.1
  101.4 0.7 copy-start.3
  101.4 1.1 copy-start.2
  187.5 13.0 %all-to-all-start.1 = ((bf16[2,4,48,768]{3,2,0,1:T(8,128)(2,1)}), bf16[2,4,48,768]{3,2,0,1:T(8,128)(2,1)S(1)}, u32[]{:S(2)}, u32[]{:S(2)}) async-start(bf16[2,4,48,768]{3,2,0,1:T(8,128)(2,1)} %copy.46), calls=%async_computation.2 | async-start | bytes 1179648 | tf_op jit(solution)/shard_map/all_to_all | solution.py:41
Sparse Core Ops, SparseCore 0:
  101.6 83.6 reduce-scatter.1
where the time goes:
time: 210 us
  waiting for transfers between devices  90.1 us (43%)
  blocking collectives  52.6 us (25%)
  matrix products  35 us (17%)
  between operations  13.6 us (6%)
  local copies, waits for them, and re-layouts  12.1 us (6%)
  starting transfers between devices  3.48 us (2%)
  other arithmetic  3.13 us (1%)
    reduce_scatter x1, waiting for transfers between devices, per_device(): lax.psum_scatter(partial_value, 'hidden', scatter_dimension=2, tiled=True)  80.6 us
    all_to_all x1, blocking collectives, per_device(): lax.all_to_all(send_rows, 'expert', split_axis=0, concat_axis=1, tiled=True)  31 us
    all_gather x1, blocking collectives, per_device(): gathered = lax.all_gather(tokens, 'hidden', axis=1, tiled=True)  21.5 us
    dot_general x1, matrix products, per_device(): jnp.einsum('erf,efd->erd', hidden_act, down_weight, preferred_element_typ...  12.9 us
    dot_general x1, matrix products, per_device(): jnp.einsum('ensd,edf->ensf', arrived, up_weight, preferred_element_type=j...  11 us
    dot_general x1, matrix products, per_device(): jnp.einsum('ensd,edf->ensf', arrived, gate_weight, preferred_element_type...  10.8 us
    all_to_all x1, waiting for transfers between devices, per_device(): lax.all_to_all(summed, 'expert', split_axis=1, concat_axis=0, tiled=True)  9.45 us
  transfers between devices with their start and end apart: 2, of which 2 were waited for; matrix products, arithmetic and copies ran while one was open for 1% of the time, Pallas kernels for 0%

commit v1 on v0

--- a/solution.py
+++ b/solution.py
@@ -24,7 +24,9 @@
     logits = jnp.dot(gathered, router_weight, preferred_element_type=jnp.float32)
     padded = jnp.concatenate([gathered, jnp.zeros((1, gathered.shape[1]), jnp.bfloat16)], axis=0)
     send_rows = padded[inverse].reshape(experts_all, 1, capacity, gathered.shape[1])
-    arrived = lax.all_to_all(send_rows, "expert", split_axis=0, concat_axis=1, tiled=True)
+    parts = jnp.split(send_rows, lax.axis_size("expert"), axis=0)
+    received = lax.all_to_all(jnp.stack(parts), "expert", 0, 0)
+    arrived = jnp.concatenate(received, axis=1)
     gate_act = jnp.einsum(
         "ensd,edf->ensf", arrived, gate_weight, preferred_element_type=jnp.float32
     )

time: 210 us -> 211 us (level)
  no operation moved by 1% of the time
where the time goes in v1:
time: 211 us; the launch traced here: 210 us
  waiting for transfers between devices  90.1 us (43%)
  blocking collectives  52.6 us (25%)
  matrix products  35 us (17%)
  between operations  13.6 us (6%)
  local copies, waits for them, and re-layouts  12.2 us (6%)
  starting transfers between devices  3.48 us (2%)
  other arithmetic  3.42 us (2%)
    reduce_scatter x1, waiting for transfers between devices, per_device(): lax.psum_scatter(partial_value, 'hidden', scatter_dimension=2, tiled=True)  80.6 us
    all_to_all x1, blocking collectives, per_device(): received = lax.all_to_all(jnp.stack(parts), 'expert', 0, 0)  31 us
    all_gather x1, blocking collectives, per_device(): gathered = lax.all_gather(tokens, 'hidden', axis=1, tiled=True)  21.5 us
    dot_general x1, matrix products, per_device(): jnp.einsum('erf,efd->erd', hidden_act, down_weight, preferred_element_typ...  12.9 us
    dot_general x1, matrix products, per_device(): jnp.einsum('ensd,edf->ensf', arrived, up_weight, preferred_element_type=j...  10.9 us
    dot_general x1, matrix products, per_device(): jnp.einsum('ensd,edf->ensf', arrived, gate_weight, preferred_element_type...  10.8 us
    all_to_all x1, waiting for transfers between devices, per_device(): lax.all_to_all(summed, 'expert', split_axis=1, concat_axis=0, tiled=True)  9.45 us
  transfers between devices with their start and end apart: 2, of which 2 were waited for; matrix products, arithmetic and copies ran while one was open for 1% of the time, Pallas kernels for 0%

profile of v1, /device:TPU:0, one launch (start us, length us, event | category | flops | bytes accessed | tf_op | source)
XLA Modules:
  0.0 210.3 jit_solution(3298297296818344044)
XLA Ops:
  6.5 0.0 copy-start
  6.5 0.0 reduce-scatter.2.cloned.1.call-start
  6.5 0.8 copy.38
  7.3 0.1 eq.29
  7.5 0.1 eq.25
  7.6 0.6 reduce-window.6
  8.2 0.2 slice_reduce_fusion
  8.5 0.1 fusion.13
  8.6 0.1 reduce_sum.15
  8.7 0.1 mul.51
  8.9 1.4 scatter_custom_fusion
  10.3 21.5 %all_gather.3 = bf16[128,3072]{1,0:T(8,128)(2,1)S(1)} all-gather(bf16[128,768]{1,0:T(8,128)(2,1)} %param.6), channel_id=1, replica_groups=mesh['groups'=2,'expert'=4,'hidden'=4] {'hidden'}, dimensions={1}, use_global_device_ids=true | all-gather | bytes 983040 | tf_op jit(solution)/shard_map/all_gather | solution.py:23
  31.8 0.0 copy-start.1
  31.8 0.9 copy-done.1
  32.7 0.1 concatenate.3
  32.8 2.9 %gather_fusion = bf16[384,3072]{1,0:T(8,128)(2,1)S(1)} fusion(bf16[129,3072]{1,0:T(8,128)(2,1)S(1)} %concatenate.3, s32[1024]{0:T(1024)S(1)} %pad_clamp_fusion.2), kind=kCustom, calls=%fused_computation | custom fusion | bytes 4720128 | tf_op jit(solution)/shard_map/gather | solution.py:26
  35.7 0.2 fusion.18
  35.9 0.3 pad_maximum_fusion
  36.2 31.0 %all_to_all.20 = bf16[4,2,1,48,3072]{4,3,1,2,0:T(8,128)(2,1)S(1)} all-to-all(bf16[4,2,1,48,3072]{4,3,1,2,0:T(8,128)(2,1)S(1)} %pad_maximum_fusion), channel_id=1, replica_groups=mesh['groups'=2,'expert'=4,'hidden'=4] {'expert'}, dimensions={0} | all-to-all | bytes 4718592 | tf_op jit(solution)/shard_map/all_to_all | solution.py:28
  67.2 10.8 %fusion.2 = f32[2,4,48,2048]{3,2,1,0:T(8,128)S(1)} fusion(bf16[2,3072,2048]{2,1,0:T(8,128)(2,1)} %param.9, bf16[4,2,1,48,3072]{4,3,1,2,0:T(8,128)(2,1)S(1)} %all_to_all.20), kind=kOutput, calls=%fused_computation.7 | convolution fusion | flops 4831838208 | bytes 30670848 | tf_op jit(solution)/shard_map/ensd,edf->ensf/dot_general | solution.py:30
  78.0 10.9 %multiply_convert_fusion = bf16[2,4,48,2048]{3,2,1,0:T(8,128)(2,1)S(1)} fusion(f32[2,4,48,2048]{3,2,1,0:T(8,128)S(1)} %fusion.2, bf16[2,3072,2048]{2,1,0:T(8,128)(2,1)} %param.10, bf16[4,2,1,48,3072]{4,3,1,2,0:T(8,128)(2,1)S(1)} %all_to_all.20), kind=kOutput, calls=%fused_computation.9 | convolution fusion | flops 4836556800 | bytes 32243712 | tf_op jit(solution)/shard_map/ensd,edf->ensf/dot_general | solution.py:33
  88.9 12.9 %fusion.20 = f32[2,192,3072]{2,1,0:T(8,128)} fusion(bf16[2,192,2048]{2,1,0:T(8,128)(2,1)S(1)} %bitcast.54, bf16[2,2048,3072]{2,1,0:T(8,128)(2,1)} %param.11), kind=kOutput, calls=%fused_computation.47 | convolution fusion | flops 4831838208 | bytes 31457280 | tf_op jit(solution)/shard_map/erf,efd->erd/dot_general | solution.py:36
  101.9 0.0 copy-start.3
  101.9 0.0 copy-start.2
  101.9 0.0 reduce-scatter.2.cloned.1.call-update
  101.9 0.7 copy-done.3
  102.6 0.1 copy.36
  102.7 0.1 reshape.113
  102.8 0.0 copy-done
  102.8 0.2 copy-done.2
  103.0 0.3 fusion.19
  103.3 1.4 gather_fusion.3
  104.7 0.1 reshape.116
  104.9 0.1 copy.37
  104.9 0.2 fusion.10
  105.1 80.6 %reduce-scatter.2.cloned.1.call-done = f32[2,192,768]{2,1,0:T(8,128)} async-done(((f32[2,192,3072]{2,1,0:T(8,128)}), f32[2,192,768]{2,1,0:T(8,128)}) %reduce-scatter.2.cloned.1.call-update) | async-done | bytes 1179664 | tf_op jit(solution)/shard_map/reduce_scatter | solution.py:39
  185.8 1.3 convert_element_type.25
  187.1 0.8 copy.42
  188.0 3.5 %all-to-all-start.1 = ((bf16[2,4,48,768]{3,2,0,1:T(8,128)(2,1)}), bf16[2,4,48,768]{3,2,0,1:T(8,128)(2,1)S(1)}, u32[]{:S(2)}, u32[]{:S(2)}) async-start(bf16[2,4,48,768]{3,2,0,1:T(8,128)(2,1)} %copy.42), calls=%async_computation.2 | async-start | bytes 1179648 | tf_op jit(solution)/shard_map/all_to_all | solution.py:43
  191.5 9.5 %all-to-all-done.1 = bf16[2,4,48,768]{3,2,0,1:T(8,128)(2,1)S(1)} async-done(((bf16[2,4,48,768]{3,2,0,1:T(8,128)(2,1)}), bf16[2,4,48,768]{3,2,0,1:T(8,128)(2,1)S(1)}, u32[]{:S(2)}, u32[]{:S(2)}) %all-to-all-start.1) | async-done | bytes 589856 | tf_op jit(solution)/shard_map/all_to_all | solution.py:43
  200.9 0.9 gather_fusion.2
  201.8 0.9 gather_fusion.1
  202.7 0.8 add_convert_fusion
  (12 shorter events, 0.1 us)
Async XLA Ops:
  6.5 96.3 %copy-start = (bf16[3072,8]{0,1:T(8,128)(2,1)S(1)}, bf16[3072,8]{0,1:T(8,128)(2,1)}, u32[]{:S(2)}) copy-start(bf16[3072,8]{0,1:T(8,128)(2,1)} %param.8) | copy-start | bytes 147460
  6.5 179.2 %reduce-scatter.2.cloned.1.call-start = ((), (), s32[]{:S(2)}) async-start(), calls=%async_computation.3 | async-start | bytes 5898240 | tf_op jit(solution)/shard_map/reduce_scatter | solution.py:39
  31.8 0.9 copy-start.1
  101.9 0.7 copy-start.3
  101.9 1.1 copy-start.2
  188.0 13.0 %all-to-all-start.1 = ((bf16[2,4,48,768]{3,2,0,1:T(8,128)(2,1)}), bf16[2,4,48,768]{3,2,0,1:T(8,128)(2,1)S(1)}, u32[]{:S(2)}, u32[]{:S(2)}) async-start(bf16[2,4,48,768]{3,2,0,1:T(8,128)(2,1)} %copy.42), calls=%async_computation.2 | async-start | bytes 1179648 | tf_op jit(solution)/shard_map/all_to_all | solution.py:43
Sparse Core Ops, SparseCore 0:
  102.0 83.6 reduce-scatter.1
